TPU v7x, 256 devices: a whole 4x4x8 slice. The times are simulated.
256 devices in a mesh: req: 32 (over z, y), tp: 8 (over x, core).
Axes of the slice: x: 4, y: 4, z: 8, core: 2. Of those that a mesh axis runs over, the one named last changes fastest.
Arguments:
- attn_heads: bfloat16 [4096, 2048], P('req', 'tp'), may hold values from -6 to 6
- residual_in: bfloat16 [4096, 4096], P('req', 'tp'), may hold values from -45 to 45
- w_out: bfloat16 [2048, 4096], P('tp'), may hold values from -0.125 to 0.125
- gain_attn: float32 [4096], P('tp'), may hold values from 0.1 to 1.9
- router: bfloat16 [4096, 8], P('tp'), may hold values from -0.09375 to 0.09375
- expert_ids: int32 [4096, 2], P('req'), may hold values from 0 to 7, all different within a row; in each aligned block of 64 rows (0 to 63, 64 to 127, ...) at most 24 rows name the same one
- lengths: int32 [32, 5], P('req'), may hold values from 1 to 64, 128 in all within a row
- placement: int32 [16], replicated, may hold values from 0 to 7, as said below
- w_gate_up: bfloat16 [32, 2, 4096, 3584], P('req', None, None, 'tp'), may hold values from -1 to 1, as said below
- w_down: bfloat16 [32, 3584, 4096], P('req', 'tp'), may hold values from -1 to 1, as said below
- gain_final: float32 [4096], P('tp'), may hold values from 0.1 to 1.9
Outputs:
- residual_out: bfloat16 [4096, 4096], P('req', 'tp')
- normed_out: bfloat16 [4096, 4096], P('req', 'tp')
Inputs may be any that keep to these rules, and one draw needn't show every extreme that they name: `expert_ids`: in each aligned block of 64 rows no expert is named by more than 24 rows, and the two experts of a row differ. `placement`: every expert is held by exactly two pairs. `w_gate_up`: index 2 s + h holds the h-th half of the hidden units of expert placement[s]; the two pairs of one expert hold equal values. `w_down`: index 2 s + h holds the h-th half of the hidden units of expert placement[s]; the two pairs of one expert hold equal values.
All inputs are finite; a program needn't handle non-finite values.
Results may differ from a plain program's by a relative error of at most 0.014.
Values may be sent and summed in bfloat16 or wider, within the bound.
A program may use at most 128 MiB of HBM per device.

v0:
```python
import jax
import jax.numpy as jnp
from jax import lax
from jax.sharding import PartitionSpec as P

epsilon = 1e-05


def on_device(
    attn_heads,
    residual_in,
    w_out,
    gain_attn,
    router,
    expert_ids,
    lengths,
    placement,
    w_gate_up,
    w_down,
    gain_final,
):
    tok_rows = attn_heads.shape[0]
    half_rows = tok_rows // 2
    feat_width = residual_in.shape[1]
    full_width = feat_width * lax.axis_size("tp")
    devices = lax.axis_size("req")
    pair_count = devices // 2
    expert_count = devices // 4
    capacity = min(half_rows, 3 * tok_rows // (2 * expert_count))
    partial_out = jnp.dot(attn_heads, w_out, preferred_element_type=jnp.float32)
    state = residual_in.astype(jnp.float32) + lax.psum_scatter(
        partial_out.astype(jnp.bfloat16), "tp", scatter_dimension=1, tiled=True
    ).astype(jnp.float32)
    router_full = router.astype(jnp.float32)
    square_sum = lax.psum(jnp.sum(state * state, axis=1), "tp")
    inverse = lax.rsqrt(square_sum / full_width + epsilon)[:, None]
    normed = state * inverse * gain_attn
    logits = lax.psum(jnp.dot(normed, router_full, precision=lax.Precision.HIGHEST), "tp")
    normed_bf = normed.astype(jnp.bfloat16)
    expert_range = jnp.arange(expert_count, dtype=jnp.int32)
    match_table = expert_ids[:, :, None] == expert_range
    chosen = jnp.sum(match_table.astype(jnp.float32) * logits[:, None, :], axis=2)
    weights = jax.nn.sigmoid(chosen - chosen[:, ::-1])
    row_index = jnp.arange(tok_rows, dtype=jnp.int32)
    live_rows = row_index < tok_rows - lengths[0, lengths.shape[1] - 1]
    held_table = (placement[:, None] == expert_range).astype(jnp.int32)
    earlier = jnp.cumsum(held_table, axis=0) - held_table
    pair_range = jnp.arange(pair_count, dtype=jnp.int32)[:, None]
    first_pair = jnp.sum(pair_range * held_table * (earlier == 0).astype(jnp.int32), axis=0)
    second_pair = jnp.sum(pair_range * held_table * (earlier == 1).astype(jnp.int32), axis=0)
    upper_half = (row_index >= half_rows)[:, None, None]
    owner_table = jnp.where(upper_half, second_pair, first_pair)
    id_hot = match_table.astype(jnp.int32) * live_rows[:, None, None].astype(jnp.int32)
    target_pair = jnp.sum(id_hot * owner_table, axis=2)
    halves_hot = id_hot.reshape(2, tok_rows, expert_count)
    running = jnp.cumsum(halves_hot, axis=1) - halves_hot
    position = jnp.sum(running * halves_hot, axis=2).reshape(tok_rows, 2)
    slot_index = jnp.where(
        live_rows[:, None], target_pair * capacity + position, pair_count * capacity
    ).reshape(-1)
    source = lax.all_gather(normed_bf, "tp", axis=1, tiled=True)
    feature_dim = source.shape[1]
    sendable = jnp.zeros((pair_count * capacity + 1, feature_dim), jnp.bfloat16)
    sendable = sendable.at[slot_index].set(jnp.repeat(source, 2, axis=0))
    per_pair = sendable[: pair_count * capacity].reshape(pair_count, 1, capacity, feature_dim)
    outgoing = jnp.broadcast_to(per_pair, (pair_count, 2, capacity, feature_dim)).reshape(
        devices, capacity, feature_dim
    )
    gate_weights = w_gate_up[0, 0]
    up_weights = w_gate_up[0, 1]
    down_weights = w_down[0]
    arrived = lax.all_to_all(outgoing, "req", split_axis=0, concat_axis=0, tiled=True)
    source_count = arrived.shape[0]
    slot_count = arrived.shape[1]
    flat_rows = arrived.reshape(source_count * slot_count, full_width)
    gate_proj = jnp.dot(flat_rows, gate_weights, preferred_element_type=jnp.float32)
    up_proj = jnp.dot(flat_rows, up_weights, preferred_element_type=jnp.float32)
    activ = (jax.nn.silu(gate_proj) * up_proj).astype(jnp.bfloat16)
    down_part = jnp.dot(activ, down_weights, preferred_element_type=jnp.float32)
    reduced = lax.psum_scatter(
        down_part.astype(jnp.bfloat16), "tp", scatter_dimension=1, tiled=True
    ).astype(jnp.float32)
    returned = lax.all_to_all(
        reduced.reshape(source_count, slot_count, feat_width).astype(jnp.bfloat16),
        "req",
        split_axis=0,
        concat_axis=0,
        tiled=True,
    ).astype(jnp.float32)
    both_halves = (
        returned.reshape(pair_count, 2, capacity, feat_width)
        .sum(axis=1)
        .reshape(pair_count * capacity, feat_width)
    )
    padded = jnp.concatenate([both_halves, jnp.zeros((1, feat_width), jnp.float32)], axis=0)
    gathered_rows = padded[slot_index].reshape(tok_rows, 2, feat_width)
    mixture = gathered_rows[:, 0] * weights[:, 0:1] + gathered_rows[:, 1] * weights[:, 1:2]
    combined = state + mixture
    final_sum = lax.psum(jnp.sum(combined * combined, axis=1), "tp")
    final_scale = lax.rsqrt(final_sum / full_width + epsilon)[:, None]
    return (
        combined.astype(jnp.bfloat16),
        (combined * final_scale * gain_final).astype(jnp.bfloat16),
    )


def solution(mesh):
    placed = (
        P("req", "tp"),
        P("req", "tp"),
        P("tp", None),
        P("tp"),
        P("tp", None),
        P("req", None),
        P("req", None),
        P(),
        P("req", None, None, "tp"),
        P("req", "tp", None),
        P("tp"),
    )
    return jax.shard_map(
        on_device,
        mesh=mesh,
        in_specs=placed,
        out_specs=(P("req", "tp"), P("req", "tp")),
        check_vma=False,
    )
```

profile of v0, /device:TPU:8, one launch (start us, length us, event | category | flops | bytes accessed | tf_op | source)
XLA Modules:
  0.0 379.3 jit_solution(5766323094708515772)
XLA Ops:
  7.3 1.5 copy-done
  8.8 2.3 convolution_convert_fusion.1
  11.1 37.7 %reduce-scatter.3.cloned.1.call-done = bf16[128,512]{1,0:T(8,128)(2,1)} async-done(((bf16[128,4096]{1,0:T(8,128)(2,1)}), bf16[128,512]{1,0:T(8,128)(2,1)}) %reduce-scatter.3.cloned.1.call-update) | async-done | bytes 131088 | tf_op jit(solution)/shard_map/reduce_scatter | solution.py:31
  48.8 1.0 multiply_reduce_fusion.1
  49.8 12.9 %psum.21 = f32[128]{0:T(128)S(1)} all-reduce(f32[128]{0:T(128)S(1)} %multiply_reduce_fusion.1), channel_id=1, replica_groups=mesh['req'=32,'tp'=8] {'tp'}, use_global_device_ids=true, to_apply=%region_8.9 | all-reduce | flops 128 | bytes 1024 | tf_op jit(solution)/shard_map/psum | solution.py:35
  62.8 1.7 fusion.23
  67.6 21.6 %all-gather.2.cloned.1.call-done = bf16[128,4096]{1,0:T(8,128)(2,1)} async-done(((bf16[128,512]{1,0:T(8,128)(2,1)}), bf16[128,4096]{1,0:T(8,128)(2,1)}) %all-gather.2.cloned.1.call-update) | async-done | bytes 1048592 | tf_op jit(solution)/shard_map/all_gather | solution.py:61
  89.3 4.7 %broadcast_in_dim.66 = bf16[128,2,4096]{2,1,0:T(2,128)(2,1)} broadcast(bf16[128,4096]{1,0:T(8,128)(2,1)} %all-gather.2.cloned.1.call-done), dimensions={0,2} | broadcast | bytes 3145728 | tf_op jit(solution)/shard_map/broadcast_in_dim | solution.py:64
  93.9 4.1 %reshape.163 = bf16[256,4096]{1,0:T(8,128)(2,1)} reshape(bf16[128,2,4096]{2,1,0:T(2,128)(2,1)} %broadcast_in_dim.66) | data formatting | bytes 4194304 | tf_op jit(solution)/shard_map/reshape | solution.py:64
  98.0 6.6 %scatter_custom_fusion = bf16[385,4096]{1,0:T(8,128)(2,1)} fusion(s32[256]{0:T(256)S(1)} %bitcast.58, bf16[256,4096]{1,0:T(8,128)(2,1)} %reshape.163, bf16[]{:T(256)} %constant.14.clone.1), kind=kCustom, calls=%fused_computation.11 | custom fusion | bytes 3154432 | tf_op jit(solution)/shard_map/scatter | solution.py:64
  104.6 1.9 slice-done
  106.5 0.8 broadcast_in_dim.68
  107.3 151.0 %all_to_all.10 = bf16[32,24,4096]{2,1,0:T(8,128)(2,1)S(1)} all-to-all(bf16[32,24,4096]{2,1,0:T(8,128)(2,1)S(1)} %bitcast.51), channel_id=1, replica_groups=mesh['req'=32,'tp'=8] {'req'}, dimensions={0} | all-to-all | bytes 12582912 | tf_op jit(solution)/shard_map/all_to_all | solution.py:72
  258.3 2.7 copy-done.1
  261.0 4.2 %fusion.3 = f32[768,448]{0,1:T(8,128)} fusion(bf16[768,4096]{1,0:T(8,128)(2,1)S(1)} %bitcast.53, bf16[1,2,4096,448]{2,3,1,0:T(8,128)(2,1)S(1)} %bitcast.61), kind=kOutput, calls=%fused_computation.7 | convolution fusion | flops 2818572288 | bytes 11337728 | tf_op jit(solution)/shard_map/dot_general | solution.py:76
  265.2 16.3 %convolution_convert_fusion = bf16[768,4096]{1,0:T(8,128)(2,1)} fusion(bf16[1,448,4096]{2,1,0:T(8,128)(2,1)} %param.20, bf16[768,4096]{1,0:T(8,128)(2,1)} %bitcast.54, bf16[1,2,4096,448]{2,3,1,0:T(8,128)(2,1)} %param.19, f32[768,448]{0,1:T(8,128)} %fusion.3), kind=kOutput, calls=%fused_computation.2 | convolution fusion | flops 5642354688 | bytes 21299200 | tf_op jit(solution)/shard_map/dot_general | solution.py:79
  281.5 40.5 %reduce-scatter.5.cloned.1.call-done = bf16[768,512]{1,0:T(8,128)(2,1)} async-done(((bf16[768,4096]{1,0:T(8,128)(2,1)}), bf16[768,512]{1,0:T(8,128)(2,1)}) %reduce-scatter.5.cloned.1.call-update) | async-done | bytes 786448 | tf_op jit(solution)/shard_map/reduce_scatter | solution.py:80
  322.0 10.2 %all-to-all-start.1 = ((bf16[32,24,512]{2,1,0:T(8,128)(2,1)}), bf16[32,24,512]{2,1,0:T(8,128)(2,1)S(1)}, u32[]{:S(2)}, u32[]{:S(2)}) async-start(bf16[32,24,512]{2,1,0:T(8,128)(2,1)} %bitcast.56), calls=%async_computation.3 | async-start | bytes 1572864 | tf_op jit(solution)/shard_map/all_to_all | solution.py:83
  333.1 13.9 %psum.22 = f32[128,8]{0,1:T(8,128)S(1)} all-reduce(f32[128,8]{0,1:T(8,128)S(1)} %fusion.22), channel_id=1, replica_groups=mesh['req'=32,'tp'=8] {'tp'}, use_global_device_ids=true, to_apply=%region_12.13 | all-reduce | flops 1024 | bytes 8192 | tf_op jit(solution)/shard_map/psum | solution.py:38
  347.6 6.5 %all-to-all-done.1 = bf16[32,24,512]{2,1,0:T(8,128)(2,1)S(1)} async-done(((bf16[32,24,512]{2,1,0:T(8,128)(2,1)}), bf16[32,24,512]{2,1,0:T(8,128)(2,1)S(1)}, u32[]{:S(2)}, u32[]{:S(2)}) %all-to-all-start.1) | async-done | bytes 786464 | tf_op jit(solution)/shard_map/all_to_all | solution.py:83
  354.3 1.1 gather_fusion
  356.1 1.1 multiply_reduce_fusion
  357.3 14.1 %psum.23 = f32[128]{0:T(128)S(1)} all-reduce(f32[128]{0:T(128)S(1)} %get-tuple-element.4), channel_id=1, replica_groups=mesh['req'=32,'tp'=8] {'tp'}, use_global_device_ids=true, to_apply=%region_15.16 | all-reduce | flops 128 | bytes 1024 | tf_op jit(solution)/shard_map/psum | solution.py:99
  371.4 1.4 multiply_convert_fusion
  (62 shorter events, 5.1 us)
Async XLA Ops:
  7.2 1.6 copy-start
  7.2 41.6 %copy-start.2 = (bf16[128,512]{1,0:T(8,128)(2,1)S(1)}, bf16[128,512]{1,0:T(8,128)(2,1)}, u32[]{:S(2)}) copy-start(bf16[128,512]{1,0:T(8,128)(2,1)} %param.12) | copy-start | bytes 393220
  7.2 55.6 %copy-start.5 = (f32[512]{0:T(512)S(1)}, f32[512]{0:T(512)}, u32[]{:S(2)}) copy-start(f32[512]{0:T(512)} %param.14) | copy-start | bytes 6148
  7.2 57.3 %copy-start.8 = (s32[1,5]{1,0:T(1,128)S(1)}, s32[1,5]{1,0:T(1,128)}, u32[]{:S(2)}) copy-start(s32[1,5]{1,0:T(1,128)} %param.17) | copy-start | bytes 64
  7.2 58.8 %copy-start.4 = (s32[128,2]{0,1:T(2,128)S(1)}, s32[128,2]{0,1:T(2,128)}, u32[]{:S(2)}) copy-start(s32[128,2]{0,1:T(2,128)} %param.16) | copy-start | bytes 3076
  7.2 59.4 %copy-start.6 = (s32[16]{0:T(128)S(1)}, s32[16]{0:T(128)}, u32[]{:S(2)}) copy-start(s32[16]{0:T(128)} %param.18) | copy-start | bytes 196
  7.2 41.6 %reduce-scatter.3.cloned.1.call-start = ((), (), s32[]{:S(2)}) async-start(), calls=%async_computation.4 | async-start | bytes 1179648 | tf_op jit(solution)/shard_map/reduce_scatter | solution.py:31
  11.1 78.2 %all-gather.2.cloned.1.call-start = ((), (), s32[]{:S(2)}) async-start(), calls=%async_computation.5 | async-start | bytes 1179648 | tf_op jit(solution)/shard_map/all_gather | solution.py:61
  64.4 257.6 %reduce-scatter.5.cloned.1.call-start = ((), (), s32[]{:S(2)}) async-start(), calls=%async_computation.6 | async-start | bytes 7077888 | tf_op jit(solution)/shard_map/reduce_scatter | solution.py:80
  104.6 1.9 slice-start
  106.5 154.5 %slice-start.1 = ((s8[7340032]{0:T(1024)(128)(4,1)}), s8[3145728]{0:T(1024)(128)(4,1)S(1)}, s32[]{:S(2)}) async-start(s8[7340032]{0:T(1024)(128)(4,1)} %bitcast.60), calls=%async_computation.8 | async-start | bytes 6291456
  107.3 153.7 %slice-start.2 = ((s8[7340032]{0:T(1024)(128)(4,1)}), s8[4194304]{0:T(1024)(128)(4,1)S(1)}, s32[]{:S(2)}) async-start(s8[7340032]{0:T(1024)(128)(4,1)} %bitcast.60), calls=%async_computation.9 | async-start | bytes 8388608
  258.3 2.7 copy-start.1
  281.5 51.3 %copy-start.3 = (bf16[128,512]{1,0:T(8,128)(2,1)S(1)}, bf16[128,512]{1,0:T(8,128)(2,1)}, u32[]{:S(2)}) copy-start(bf16[128,512]{1,0:T(8,128)(2,1)} %reduce-scatter.3.cloned.1.call-done) | copy-start | bytes 393220
  281.5 51.3 %copy-start.7 = (bf16[512,8]{0,1:T(8,128)(2,1)S(1)}, bf16[512,8]{0,1:T(8,128)(2,1)}, u32[]{:S(2)}) copy-start(bf16[512,8]{0,1:T(8,128)(2,1)} %param.15) | copy-start | bytes 24580
  322.0 32.1 %all-to-all-start.1 = ((bf16[32,24,512]{2,1,0:T(8,128)(2,1)}), bf16[32,24,512]{2,1,0:T(8,128)(2,1)S(1)}, u32[]{:S(2)}, u32[]{:S(2)}) async-start(bf16[32,24,512]{2,1,0:T(8,128)(2,1)} %bitcast.56), calls=%async_computation.3 | async-start | bytes 1572864 | tf_op jit(solution)/shard_map/all_to_all | solution.py:83
Sparse Core Ops, SparseCore 0:
  11.2 37.5 reduce-scatter.2
  64.6 24.6 all-gather.1
  281.7 40.3 reduce-scatter.4
where the time goes:
time: 380 us; the launch traced here: 379 us
  blocking collectives  192 us (51%)
  waiting for transfers between devices  106 us (28%)
  local copies, waits for them, and re-layouts  26.3 us (7%)
  matrix products  23.1 us (6%)
  between operations  14.6 us (4%)
  starting transfers between devices  10.3 us (3%)
  other arithmetic  6.89 us (2%)
    all_to_all x1, blocking collectives, on_device(): lax.all_to_all(outgoing, 'req', split_axis=0, concat_axis=0, tiled=True)  151 us
    reduce_scatter x1, waiting for transfers between devices, on_device(): lax.psum_scatter(down_part.astype(jnp.bfloat16), 'tp', scatter_dimension=...  40.5 us
    reduce_scatter x1, waiting for transfers between devices, on_device(): lax.psum_scatter(partial_out.astype(jnp.bfloat16), 'tp', scatter_dimensio...  37.7 us
    all_gather x1, waiting for transfers between devices, on_device(): source = lax.all_gather(normed_bf, 'tp', axis=1, tiled=True)  21.6 us
    dot_general x1, matrix products, on_device(): down_part = jnp.dot(activ, down_weights, preferred_element_type=jnp.float32)  16.3 us
    psum x1, blocking collectives, on_device(): final_sum = lax.psum(jnp.sum(combined * combined, axis=1), 'tp')  14.1 us
    psum x1, blocking collectives, on_device(): lax.psum(jnp.dot(normed, router_full, precision=lax.Precision.HIGHEST), '...  13.9 us
    psum x1, blocking collectives, on_device(): square_sum = lax.psum(jnp.sum(state * state, axis=1), 'tp')  12.9 us
  transfers between devices with their start and end apart: 4, of which 4 were waited for; matrix products, arithmetic and copies ran while one was open for 1% of the time, Pallas kernels for 0%

commit v1 on v0

--- a/solution.py
+++ b/solution.py
@@ -58,7 +58,10 @@
     slot_index = jnp.where(
         live_rows[:, None], target_pair * capacity + position, pair_count * capacity
     ).reshape(-1)
-    source = lax.all_gather(normed_bf, "tp", axis=1, tiled=True)
+    size = lax.axis_size("tp")
+    blocks = jnp.stack([normed_bf for _ in range(size)])
+    blocks = lax.all_to_all(blocks, "tp", split_axis=0, concat_axis=0)
+    source = jnp.concatenate(blocks, axis=1)
     feature_dim = source.shape[1]
     sendable = jnp.zeros((pair_count * capacity + 1, feature_dim), jnp.bfloat16)
     sendable = sendable.at[slot_index].set(jnp.repeat(source, 2, axis=0))

time: 380 us -> 376 us (0.989)
  waiting for transfers between devices: 106 us -> 93.3 us
  local copies, waits for them, and re-layouts: 26.3 us -> 30.1 us
    all_gather x1 -> x0, waiting for transfers between devices: 21.6 us -> none  [on_device(): source = lax.all_gather(normed_bf, 'tp', axis=1, tiled=True)]
    all_to_all x0 -> x1, waiting for transfers between devices: none -> 12.3 us  [on_device(): blocks = lax.all_to_all(blocks, 'tp', split_axis=0, concat_axis=0)]
  transfers between devices with their start and end apart: 4 -> 4, of which waited for: 4 -> 4; matrix products, arithmetic and copies ran while one was open for 1% -> 2% of each run, Pallas kernels for 0% -> 0%
where the time goes in v1:
time: 376 us
  blocking collectives  191 us (51%)
  waiting for transfers between devices  93.3 us (25%)
  local copies, waits for them, and re-layouts  30.1 us (8%)
  matrix products  23.1 us (6%)
  between operations  14.9 us (4%)
  starting transfers between devices  13.8 us (4%)
  other arithmetic  9.19 us (2%)
    all_to_all x1, blocking collectives, on_device(): lax.all_to_all(outgoing, 'req', split_axis=0, concat_axis=0, tiled=True)  150 us
    reduce_scatter x1, waiting for transfers between devices, on_device(): lax.psum_scatter(down_part.astype(jnp.bfloat16), 'tp', scatter_dimension=...  40.1 us
    reduce_scatter x1, waiting for transfers between devices, on_device(): lax.psum_scatter(partial_out.astype(jnp.bfloat16), 'tp', scatter_dimensio...  34.5 us
    dot_general x1, matrix products, on_device(): down_part = jnp.dot(activ, down_weights, preferred_element_type=jnp.float32)  16.3 us
    psum x1, blocking collectives, on_device(): final_sum = lax.psum(jnp.sum(combined * combined, axis=1), 'tp')  14.1 us
    psum x1, blocking collectives, on_device(): lax.psum(jnp.dot(normed, router_full, precision=lax.Precision.HIGHEST), '...  13.9 us
    psum x1, blocking collectives, on_device(): square_sum = lax.psum(jnp.sum(state * state, axis=1), 'tp')  12.9 us
    all_to_all x1, waiting for transfers between devices, on_device(): blocks = lax.all_to_all(blocks, 'tp', split_axis=0, concat_axis=0)  12.3 us
  transfers between devices with their start and end apart: 4, of which 4 were waited for; matrix products, arithmetic and copies ran while one was open for 2% of the time, Pallas kernels for 0%

profile of v1, /device:TPU:8, one launch (start us, length us, event | category | flops | bytes accessed | tf_op | source)
XLA Modules:
  0.0 375.7 jit_solution(1695460836093451233)
XLA Ops:
  7.3 1.5 copy-done
  8.8 2.3 convolution_convert_fusion.1
  14.3 34.5 %reduce-scatter.3.cloned.1.call-done = bf16[128,512]{1,0:T(8,128)(2,1)} async-done(((bf16[128,4096]{1,0:T(8,128)(2,1)}), bf16[128,512]{1,0:T(8,128)(2,1)}) %reduce-scatter.3.cloned.1.call-update) | async-done | bytes 131088 | tf_op jit(solution)/shard_map/reduce_scatter | solution.py:31
  49.8 12.9 %psum.21 = f32[128]{0:T(128)S(1)} all-reduce(f32[128]{0:T(128)S(1)} %multiply_reduce_fusion.1), channel_id=1, replica_groups=mesh['req'=32,'tp'=8] {'tp'}, use_global_device_ids=true, to_apply=%region_8.9 | all-reduce | flops 128 | bytes 1024 | tf_op jit(solution)/shard_map/psum | solution.py:35
  65.4 3.6 all-to-all-start
  72.5 12.3 %all-to-all-done = bf16[8,128,512]{2,1,0:T(8,128)(2,1)S(1)} async-done(((bf16[8,128,512]{2,1,0:T(8,128)(2,1)}), bf16[8,128,512]{2,1,0:T(8,128)(2,1)S(1)}, u32[]{:S(2)}, u32[]{:S(2)}) %all-to-all-start) | async-done | bytes 1048608 | tf_op jit(solution)/shard_map/all_to_all | solution.py:63
  84.8 1.3 copy.34
  86.1 1.5 copy.35
  87.6 3.5 broadcast_in_dim.66
  91.1 4.1 %reshape.173 = bf16[256,4096]{1,0:T(8,128)(2,1)} reshape(bf16[128,2,4096]{2,1,0:T(2,128)(2,1)} %broadcast_in_dim.66) | data formatting | bytes 4194304 | tf_op jit(solution)/shard_map/reshape | solution.py:67
  95.2 6.6 %scatter_custom_fusion = bf16[385,4096]{1,0:T(8,128)(2,1)} fusion(s32[256]{0:T(256)S(1)} %bitcast.62, bf16[256,4096]{1,0:T(8,128)(2,1)} %reshape.173, bf16[]{:T(256)} %constant.14.clone.1), kind=kCustom, calls=%fused_computation.11 | custom fusion | bytes 3154432 | tf_op jit(solution)/shard_map/scatter | solution.py:67
  101.7 1.9 slice-done
  104.4 150.4 %all_to_all.15 = bf16[32,24,4096]{2,1,0:T(8,128)(2,1)S(1)} all-to-all(bf16[32,24,4096]{2,1,0:T(8,128)(2,1)S(1)} %bitcast.54), channel_id=1, replica_groups=mesh['req'=32,'tp'=8] {'req'}, dimensions={0} | all-to-all | bytes 12582912 | tf_op jit(solution)/shard_map/all_to_all | solution.py:75
  254.8 2.7 copy-done.1
  257.5 4.2 %fusion.3 = f32[768,448]{0,1:T(8,128)} fusion(bf16[768,4096]{1,0:T(8,128)(2,1)S(1)} %bitcast.56, bf16[1,2,4096,448]{2,3,1,0:T(8,128)(2,1)S(1)} %bitcast.65), kind=kOutput, calls=%fused_computation.7 | convolution fusion | flops 2818572288 | bytes 11337728 | tf_op jit(solution)/shard_map/dot_general | solution.py:79
  261.7 16.3 %convolution_convert_fusion = bf16[768,4096]{1,0:T(8,128)(2,1)} fusion(bf16[1,448,4096]{2,1,0:T(8,128)(2,1)} %param.20, bf16[768,4096]{1,0:T(8,128)(2,1)} %bitcast.57, bf16[1,2,4096,448]{2,3,1,0:T(8,128)(2,1)} %param.19, f32[768,448]{0,1:T(8,128)} %fusion.3), kind=kOutput, calls=%fused_computation.2 | convolution fusion | flops 5642354688 | bytes 21299200 | tf_op jit(solution)/shard_map/dot_general | solution.py:82
  278.0 40.1 %reduce-scatter.5.cloned.1.call-done = bf16[768,512]{1,0:T(8,128)(2,1)} async-done(((bf16[768,4096]{1,0:T(8,128)(2,1)}), bf16[768,512]{1,0:T(8,128)(2,1)}) %reduce-scatter.5.cloned.1.call-update) | async-done | bytes 786448 | tf_op jit(solution)/shard_map/reduce_scatter | solution.py:83
  318.1 10.2 %all-to-all-start.2 = ((bf16[32,24,512]{2,1,0:T(8,128)(2,1)}), bf16[32,24,512]{2,1,0:T(8,128)(2,1)S(1)}, u32[]{:S(2)}, u32[]{:S(2)}) async-start(bf16[32,24,512]{2,1,0:T(8,128)(2,1)} %bitcast.60), calls=%async_computation.4 | async-start | bytes 1572864 | tf_op jit(solution)/shard_map/all_to_all | solution.py:86
  329.1 13.9 %psum.22 = f32[128,8]{0,1:T(8,128)S(1)} all-reduce(f32[128,8]{0,1:T(8,128)S(1)} %fusion.22), channel_id=1, replica_groups=mesh['req'=32,'tp'=8] {'tp'}, use_global_device_ids=true, to_apply=%region_12.13 | all-reduce | flops 1024 | bytes 8192 | tf_op jit(solution)/shard_map/psum | solution.py:38
  343.7 6.5 %all-to-all-done.2 = bf16[32,24,512]{2,1,0:T(8,128)(2,1)S(1)} async-done(((bf16[32,24,512]{2,1,0:T(8,128)(2,1)}), bf16[32,24,512]{2,1,0:T(8,128)(2,1)S(1)}, u32[]{:S(2)}, u32[]{:S(2)}) %all-to-all-start.2) | async-done | bytes 786464 | tf_op jit(solution)/shard_map/all_to_all | solution.py:86
  350.4 1.1 gather_fusion
  352.2 1.1 multiply_reduce_fusion
  353.3 14.1 %psum.23 = f32[128]{0:T(128)S(1)} all-reduce(f32[128]{0:T(128)S(1)} %get-tuple-element.4), channel_id=1, replica_groups=mesh['req'=32,'tp'=8] {'tp'}, use_global_device_ids=true, to_apply=%region_15.16 | all-reduce | flops 128 | bytes 1024 | tf_op jit(solution)/shard_map/psum | solution.py:102
  367.4 1.4 multiply_convert_fusion
  (72 shorter events, 13.1 us)
Async XLA Ops:
  7.2 1.6 copy-start
  7.2 3.9 %copy-start.12 = (s32[1,5]{1,0:T(1,128)S(1)}, s32[1,5]{1,0:T(1,128)}, u32[]{:S(2)}) copy-start(s32[1,5]{1,0:T(1,128)} %param.17) | copy-start | bytes 64
  7.2 5.4 %copy-start.4 = (s32[128,2]{0,1:T(2,128)S(1)}, s32[128,2]{0,1:T(2,128)}, u32[]{:S(2)}) copy-start(s32[128,2]{0,1:T(2,128)} %param.16) | copy-start | bytes 3076
  7.2 5.6 %copy-start.7 = (s32[16]{0:T(128)S(1)}, s32[16]{0:T(128)}, u32[]{:S(2)}) copy-start(s32[16]{0:T(128)} %param.18) | copy-start | bytes 196
  7.2 41.6 %copy-start.2 = (bf16[128,512]{1,0:T(8,128)(2,1)S(1)}, bf16[128,512]{1,0:T(8,128)(2,1)}, u32[]{:S(2)}) copy-start(bf16[128,512]{1,0:T(8,128)(2,1)} %param.12) | copy-start | bytes 393220
  7.2 56.1 %copy-start.5 = (f32[512]{0:T(512)S(1)}, f32[512]{0:T(512)}, u32[]{:S(2)}) copy-start(f32[512]{0:T(512)} %param.14) | copy-start | bytes 6148
  7.2 41.6 %reduce-scatter.3.cloned.1.call-start = ((), (), s32[]{:S(2)}) async-start(), calls=%async_computation.5 | async-start | bytes 1179648 | tf_op jit(solution)/shard_map/reduce_scatter | solution.py:31
  62.8 0.5 copy-start.9
  64.3 5.5 %copy-start.8 = (s32[8]{0:T(128)S(1)}, s32[8]{0:T(128)}, u32[]{:S(2)}) copy-start(s32[8]{0:T(128)} %get-tuple-element.2) | copy-start | bytes 100
  65.4 19.4 %all-to-all-start = ((bf16[8,128,512]{2,1,0:T(8,128)(2,1)}), bf16[8,128,512]{2,1,0:T(8,128)(2,1)S(1)}, u32[]{:S(2)}, u32[]{:S(2)}) async-start(bf16[8,128,512]{2,1,0:T(8,128)(2,1)} %stack.2), calls=%async_computation.1 | async-start | bytes 2097152 | tf_op jit(solution)/shard_map/all_to_all | solution.py:63
  68.9 249.1 %reduce-scatter.5.cloned.1.call-start = ((), (), s32[]{:S(2)}) async-start(), calls=%async_computation.6 | async-start | bytes 7077888 | tf_op jit(solution)/shard_map/reduce_scatter | solution.py:83
  101.7 1.9 slice-start
  103.6 153.8 %slice-start.1 = ((s8[7340032]{0:T(1024)(128)(4,1)}), s8[3145728]{0:T(1024)(128)(4,1)S(1)}, s32[]{:S(2)}) async-start(s8[7340032]{0:T(1024)(128)(4,1)} %bitcast.64), calls=%async_computation.8 | async-start | bytes 6291456
  104.4 153.0 %slice-start.2 = ((s8[7340032]{0:T(1024)(128)(4,1)}), s8[4194304]{0:T(1024)(128)(4,1)S(1)}, s32[]{:S(2)}) async-start(s8[7340032]{0:T(1024)(128)(4,1)} %bitcast.64), calls=%async_computation.9 | async-start | bytes 8388608
  254.8 2.7 copy-start.1
  278.0 50.9 %copy-start.3 = (bf16[128,512]{1,0:T(8,128)(2,1)S(1)}, bf16[128,512]{1,0:T(8,128)(2,1)}, u32[]{:S(2)}) copy-start(bf16[128,512]{1,0:T(8,128)(2,1)} %reduce-scatter.3.cloned.1.call-done) | copy-start | bytes 393220
  278.0 50.9 %copy-start.6 = (f32[512]{0:T(512)S(1)}, f32[512]{0:T(512)}, u32[]{:S(2)}) copy-start(f32[512]{0:T(512)} %param.14) | copy-start | bytes 6148
  278.0 50.9 %copy-start.10 = (f32[128]{0:T(128)S(1)}, f32[128]{0:T(128)}, u32[]{:S(2)}) copy-start(f32[128]{0:T(128)} %copy-done.9) | copy-start | bytes 1540
  278.0 50.9 %copy-start.11 = (bf16[512,8]{0,1:T(8,128)(2,1)S(1)}, bf16[512,8]{0,1:T(8,128)(2,1)}, u32[]{:S(2)}) copy-start(bf16[512,8]{0,1:T(8,128)(2,1)} %param.15) | copy-start | bytes 24580
  318.1 32.1 %all-to-all-start.2 = ((bf16[32,24,512]{2,1,0:T(8,128)(2,1)}), bf16[32,24,512]{2,1,0:T(8,128)(2,1)S(1)}, u32[]{:S(2)}, u32[]{:S(2)}) async-start(bf16[32,24,512]{2,1,0:T(8,128)(2,1)} %bitcast.60), calls=%async_computation.4 | async-start | bytes 1572864 | tf_op jit(solution)/shard_map/all_to_all | solution.py:86
Sparse Core Ops, SparseCore 0:
  11.2 37.5 reduce-scatter.2
  278.1 39.8 reduce-scatter.4
